TPU v7x, 32 devices: a whole 2x2x4 slice. The times are simulated.
32 devices in a mesh: grp: 2 (over y), trade: 4 (over z), date: 2 (over x), path: 2 (over core).
Axes of the slice: x: 2, y: 2, z: 4, core: 2. Of those that a mesh axis runs over, the one named last changes fastest.
Arguments:
- driver_increments: float32 [16, 256, 128], P(('grp', 'date'), 'path'), parts along dimension 0, may hold values from -4 to 4
- persistence_ratio: float32 [16, 128], P(('grp', 'date')), parts along dimension 0, may hold values from 0 to 1, as said below
- deal_sensitivity: bfloat16 [128, 65536], P(None, ('grp', 'trade')), parts along dimension 1, may hold values from -0.5 to 0.5
- signed_notional: float32 [65536], P(('grp', 'trade')), parts along dimension 0, may hold values from -0.4 to 0.4
- batch_obligor: int32 [512], P(('grp', 'trade')), parts along dimension 0, may hold values from 0 to 127, as said below
- collateral_ceiling: float32 [256], P(('grp', 'trade')), parts along dimension 0, may hold values from -1 to 1
- default_discount_mass: float32 [16, 128], P(('grp', 'date'), 'trade'), parts along dimension 0, may hold values from 0.1 to 1
Outputs:
- exposure_profile: float32 [16, 128], P(('grp', 'date'), 'trade'), parts along dimension 0
- shock_gradient: float32 [16, 256, 128], P(('grp', 'date'), 'path'), parts along dimension 0
There are 2 independent parts, one for each index of `grp`. A program takes and returns all parts, laid end to end along the dimension named above; each array names one. Nothing has to cross between parts.
Inputs may be any that keep to these rules, and one draw needn't show every extreme that they name: `persistence_ratio`: strictly between 0 and 1. `batch_obligor`: counterparty c belongs to trade shard c // 32. Of the 64 trade blocks of one trade shard, at most 32 have counterparties on any one trade shard, and in every trade shard some counterparty shard receives exactly 32 of them.
All inputs are finite; a program needn't handle non-finite values.
Results may differ from a plain program's by a relative error of at most 0.0019.
Values sent between devices are 32-bit elements; how exact they have to be, the bound alone decides.
No kernel may reach another device: no remote copies, remote signals or barrier semaphores. Data moves between devices by JAX's collectives and lax.ppermute only.
A program may use at most 64 MiB of HBM per device.

v0:
```python
import jax
import jax.numpy as jnp
from jax import lax
from jax.sharding import PartitionSpec as P

block_width = 128
cluster_extent = 512
highest = lax.Precision.HIGHEST


def entering(value, axis, combine, identity, reverse):
    length, index = (lax.axis_size(axis), lax.axis_index(axis))
    everything = jax.tree.map(lambda part: lax.all_gather(part, axis), value)
    start = jax.tree.map(
        lambda part, zero: jnp.broadcast_to(jnp.asarray(zero, part.dtype), part.shape),
        value,
        identity,
    )

    def hop(k, before):
        at = length - 1 - k if reverse else k
        reached = at > index if reverse else at < index
        new = combine(before, jax.tree.map(lambda part: part[at], everything))
        return jax.tree.map(lambda a, b: jnp.where(reached, a, b), new, before)

    return lax.fori_loop(0, length, hop, start)


def compose(earlier, later):
    return (later[0] * earlier[0], later[0] * earlier[1] + later[1])


def reverse_chain(direct, persistence_ratio):
    date_count = direct.shape[0]
    factor_gain = jnp.ones((direct.shape[2],), jnp.float32)
    message = jnp.zeros(direct.shape[1:], jnp.float32)
    for date_step in reversed(range(date_count)):
        message = persistence_ratio[date_step][None, :] * (direct[date_step] + message)
        factor_gain = persistence_ratio[date_step] * factor_gain
    identity = (jnp.ones_like(factor_gain), jnp.zeros_like(message))
    _, arriving = entering((factor_gain, message), "date", compose, identity, True)
    adjoints = []
    message = arriving
    for date_step in reversed(range(date_count)):
        adjoint = direct[date_step] + message
        adjoints.append(adjoint)
        message = persistence_ratio[date_step][None, :] * adjoint
    return jnp.stack(adjoints[::-1])


def shards(
    driver_increments,
    persistence_ratio,
    deal_sensitivity,
    signed_notional,
    batch_obligor,
    collateral_ceiling,
    default_discount_mass,
):
    date_count, path_count, factor_count = driver_increments.shape
    factor_gain = jnp.ones((factor_count,), jnp.float32)
    carried = jnp.zeros((path_count, factor_count), jnp.float32)
    for date_step in range(date_count):
        carried = persistence_ratio[date_step][None, :] * carried + driver_increments[date_step]
        factor_gain = persistence_ratio[date_step] * factor_gain
    identity = (jnp.ones_like(factor_gain), jnp.zeros_like(carried))
    _, arriving = entering((factor_gain, carried), "date", compose, identity, False)
    states = []
    carried = arriving
    for date_step in range(date_count):
        carried = persistence_ratio[date_step][None, :] * carried + driver_increments[date_step]
        states.append(carried)
    row_count = date_count * path_count
    state_bf = jnp.stack(states).reshape(row_count, factor_count).astype(jnp.bfloat16)
    deal_ordinal = deal_sensitivity.shape[1]
    block_count = deal_ordinal // block_width
    cluster_ordinal = deal_ordinal // cluster_extent
    per_group = cluster_extent // block_width

    def value_group(group_index, block_sums):
        opening_offset = group_index * cluster_extent
        sensitivity_portion = lax.dynamic_slice_in_dim(
            deal_sensitivity, opening_offset, cluster_extent, 1
        )
        size_part = lax.dynamic_slice_in_dim(signed_notional, opening_offset, cluster_extent, 0)
        linear = jnp.dot(state_bf, sensitivity_portion, preferred_element_type=jnp.float32)
        trade_value = jax.nn.softplus(linear) * size_part[None, :]
        summed = trade_value.reshape(row_count, per_group, block_width).sum(axis=2)
        return lax.dynamic_update_slice_in_dim(block_sums, summed.T, group_index * per_group, 0)

    block_sums = lax.fori_loop(
        0, cluster_ordinal, value_group, jnp.zeros((block_count, row_count), jnp.float32)
    )
    cpty_dev = collateral_ceiling.shape[0]
    shard_count = lax.axis_size("trade")
    ownership = (
        batch_obligor[:, None] == jnp.arange(cpty_dev * shard_count, dtype=jnp.int32)[None, :]
    ).astype(jnp.float32)
    partial_value = lax.dot_general(
        ownership, block_sums, (((0,), (0,)), ((), ())), precision=highest
    )
    netted = lax.psum_scatter(partial_value, "trade", scatter_dimension=0, tiled=True)
    shifted = netted - collateral_ceiling[:, None]
    exposure = jax.nn.softplus(shifted).reshape(cpty_dev, date_count, path_count)
    path_total = lax.psum(jnp.sum(exposure, axis=2).T, "path")
    exposure_profile = path_total / (path_count * lax.axis_size("path"))
    net_adjoint = (
        default_discount_mass.T[:, :, None]
        * jax.nn.sigmoid(shifted).reshape(cpty_dev, date_count, path_count)
    ).reshape(cpty_dev, row_count)
    gathered = lax.all_gather(net_adjoint, "trade", axis=0, tiled=True)
    block_adjoint = jnp.dot(ownership, gathered, precision=highest)

    def pull_group(group_index, running):
        opening_offset = group_index * cluster_extent
        sensitivity_portion = lax.dynamic_slice_in_dim(
            deal_sensitivity, opening_offset, cluster_extent, 1
        )
        size_part = lax.dynamic_slice_in_dim(signed_notional, opening_offset, cluster_extent, 0)
        linear = jnp.dot(state_bf, sensitivity_portion, preferred_element_type=jnp.float32)
        slope_term = jax.nn.sigmoid(linear) * size_part[None, :]
        upstream = lax.dynamic_slice_in_dim(block_adjoint, group_index * per_group, per_group, 0)
        value_adjoint = (
            (upstream.T[:, :, None] * slope_term.reshape(row_count, per_group, block_width))
            .reshape(row_count, cluster_extent)
            .astype(jnp.bfloat16)
        )
        product = lax.dot_general(
            value_adjoint,
            sensitivity_portion,
            (((1,), (1,)), ((), ())),
            preferred_element_type=jnp.float32,
        )
        return running + product

    direct = lax.fori_loop(
        0, cluster_ordinal, pull_group, jnp.zeros((row_count, factor_count), jnp.float32)
    )
    direct = direct.reshape(date_count, path_count, factor_count)
    summed = lax.psum(direct, "trade")
    shock_gradient = reverse_chain(summed, persistence_ratio)
    return (exposure_profile, shock_gradient)


def solution(mesh):
    return jax.shard_map(
        shards,
        mesh=mesh,
        in_specs=(
            P(("grp", "date"), "path", None),
            P(("grp", "date"), None),
            P(None, ("grp", "trade")),
            P(("grp", "trade")),
            P(("grp", "trade")),
            P(("grp", "trade")),
            P(("grp", "date"), "trade"),
        ),
        out_specs=(P(("grp", "date"), "trade"), P(("grp", "date"), "path", None)),
        check_vma=False,
    )
```

profile of v0, /device:TPU:0, one launch (start us, length us, event | category | flops | bytes accessed | tf_op | source)
XLA Modules:
  0.0 200.2 jit_solution(7079904627721618631)
XLA Ops:
  7.2 0.8 multiply_bitcast_fusion
  8.8 5.1 %all-gather = f32[2,1,128]{2,1,0:T(1,128)S(1)} all-gather(f32[1,1,128]{2,1,0:T(1,128)S(1)} %get-tuple-element.550), channel_id=1, replica_groups=mesh['grp'=2,'trade'=4,'date'=2,'path'=2] {'date'}, dimensions={0}, use_global_device_ids=true | all-gather | bytes 1536 | tf_op jit(solution)/shard_map/all_gather | solution.py:13
  13.8 1.0 multiply_add_fusion
  14.8 4.9 %all_gather.20 = f32[2,128,128]{2,1,0:T(8,128)S(1)} all-gather(f32[1,128,128]{2,1,0:T(8,128)S(1)} %multiply_add_fusion), channel_id=1, replica_groups=mesh['grp'=2,'trade'=4,'date'=2,'path'=2] {'date'}, dimensions={0}, use_global_device_ids=true | all-gather | bytes 196608 | tf_op jit(solution)/shard_map/all_gather | solution.py:13
  19.9 0.9 convert_bitcast_fusion.1
  20.9 41.0 %while.57 = (s32[]{:T(128)}, f32[64,512]{1,0:T(8,128)S(1)}, bf16[128,8192]{1,0:T(8,128)(2,1)}, bf16[512,128]{1,0:T(8,128)(2,1)S(1)}, f32[8192]{0:T(1024)}, /*ind...) while((s32[]{:T(128)}, f32[64,512]{1,0:T(8,128)S(1)}, ...), condition=%wide.region_4.5_spmd, body=%wide.region_2.4_spmd.sunk | while | flops 69203976 | bytes 293085 | solution.py:91
  20.9 0.8 dynamic_slice.97
  21.7 1.8 bitcast_reduce_fusion.2
  23.5 0.8 dynamic_slice.97
  24.2 1.8 bitcast_reduce_fusion.2
  26.0 0.8 dynamic_slice.97
  26.8 1.8 bitcast_reduce_fusion.2
  28.6 0.8 dynamic_slice.97
  29.4 1.8 bitcast_reduce_fusion.2
  31.1 0.8 dynamic_slice.97
  31.9 1.8 bitcast_reduce_fusion.2
  33.7 0.8 dynamic_slice.97
  34.5 1.8 bitcast_reduce_fusion.2
  36.3 0.8 dynamic_slice.97
  37.0 1.8 bitcast_reduce_fusion.2
  38.8 0.8 dynamic_slice.97
  39.6 1.7 bitcast_reduce_fusion.2
  41.4 0.8 dynamic_slice.97
  42.2 1.8 bitcast_reduce_fusion.2
  43.9 0.8 dynamic_slice.97
  44.7 1.8 bitcast_reduce_fusion.2
  46.5 0.8 dynamic_slice.97
  47.3 1.8 bitcast_reduce_fusion.2
  49.1 0.8 dynamic_slice.97
  49.8 1.7 bitcast_reduce_fusion.2
  52.4 1.8 bitcast_reduce_fusion.2
  55.0 1.8 bitcast_reduce_fusion.2
  56.8 0.8 dynamic_slice.97
  57.5 1.8 bitcast_reduce_fusion.2
  60.1 1.8 bitcast_reduce_fusion.2
  61.9 1.1 fusion.27
  63.1 21.4 %reduce-scatter.2.cloned.1.call-done = f32[32,512]{1,0:T(8,128)} async-done(((f32[128,512]{1,0:T(8,128)}), f32[32,512]{1,0:T(8,128)}) %reduce-scatter.2.cloned.1.call-update) | async-done | bytes 65552 | tf_op jit(solution)/shard_map/reduce_scatter | solution.py:102
  84.6 1.0 bitcast_multiply_fusion
  85.6 13.8 %all_gather.21 = f32[128,512]{1,0:T(8,128)S(1)} all-gather(f32[32,512]{1,0:T(8,128)S(1)} %get-tuple-element.544), channel_id=1, replica_groups=mesh['grp'=2,'trade'=4,'date'=2,'path'=2] {'trade'}, dimensions={0}, use_global_device_ids=true | all-gather | bytes 327680 | tf_op jit(solution)/shard_map/all_gather | solution.py:111
  99.7 50.3 %while.59 = (s32[]{:T(128)}, f32[512,128]{1,0:T(8,128)S(1)}, f32[64,512]{1,0:T(8,128)S(1)}, bf16[128,8192]{1,0:T(8,128)(2,1)}, bf16[512,128]{1,0:T(8,128)(2,1)S(...) while((s32[]{:T(128)}, f32[512,128]{1,0:T(8,128)S(1)}, ...), condition=%wide.region_9.10_spmd.clone, body=%wide.region_8.9_spmd.clone.sunk | while | flops 135921680 | bytes 3063530 | solution.py:136
  101.3 1.6 fusion.50
  104.4 1.6 fusion.50
  107.6 1.6 fusion.50
  110.7 1.6 fusion.50
  113.8 1.6 fusion.50
  117.0 1.6 fusion.50
  120.1 1.6 fusion.50
  123.3 1.6 fusion.50
  126.4 1.6 fusion.50
  129.5 1.6 fusion.50
  132.7 1.6 fusion.50
  135.8 1.6 fusion.50
  139.0 1.6 fusion.50
  142.1 1.6 fusion.50
  145.3 1.6 fusion.50
  147.7 0.8 dynamic_slice.103
  148.4 1.6 fusion.50
  150.8 4.2 %all-gather.1 = f32[2,1,128]{2,1,0:T(1,128)S(1)} all-gather(f32[1,1,128]{2,1,0:T(1,128)S(1)} %get-tuple-element.546), channel_id=1, replica_groups=mesh['grp'=2,'trade'=4,'date'=2,'path'=2] {'date'}, dimensions={0}, use_global_device_ids=true | all-gather | bytes 1536 | tf_op jit(solution)/shard_map/all_gather | solution.py:13
  155.1 3.4 %psum.14 = f32[4,32]{0,1:T(8,128)S(1)} all-reduce(f32[4,32]{0,1:T(8,128)S(1)} %bitcast.153), channel_id=1, replica_groups=mesh['grp'=2,'trade'=4,'date'=2,'path'=2] {'path'}, use_global_device_ids=true, to_apply=%region_7.8 | all-reduce | flops 128 | bytes 1024 | tf_op jit(solution)/shard_map/psum | solution.py:105
  159.1 25.7 %all-reduce.2.cloned.1.call-done = f32[4,128,128]{2,1,0:T(8,128)} async-done(((f32[4,128,128]{2,1,0:T(8,128)}), f32[4,128,128]{2,1,0:T(8,128)}) %all-reduce.2.cloned.1.call-update) | async-done | bytes 262160 | tf_op jit(solution)/shard_map/psum | solution.py:140
  184.8 1.0 add_multiply_fusion
  185.8 4.9 %all_gather.23 = f32[2,128,128]{2,1,0:T(8,128)S(1)} all-gather(f32[1,128,128]{2,1,0:T(8,128)S(1)} %add_multiply_fusion), channel_id=1, replica_groups=mesh['grp'=2,'trade'=4,'date'=2,'path'=2] {'date'}, dimensions={0}, use_global_device_ids=true | all-gather | bytes 196608 | tf_op jit(solution)/shard_map/all_gather | solution.py:13
  190.8 1.0 fusion.23
  191.8 0.9 fusion.29
  (121 shorter events, 30.0 us)
Async XLA Ops:
  7.2 13.6 %copy-start = (f32[4,128,128]{2,1,0:T(8,128)S(1)}, f32[4,128,128]{2,1,0:T(8,128)}, u32[]{:S(2)}) copy-start(f32[4,128,128]{2,1,0:T(8,128)} %param.15) | copy-start | bytes 786436
  7.2 77.3 %reduce-scatter.2.cloned.1.call-start = ((), (), s32[]{:S(2)}) async-start(), calls=%async_computation.1 | async-start | bytes 327680 | tf_op jit(solution)/shard_map/reduce_scatter | solution.py:102
  20.8 41.0 %copy-start.2 = (s32[64]{0:T(128)S(1)}, s32[64]{0:T(128)}, u32[]{:S(2)}) copy-start(s32[64]{0:T(128)} %param.19) | copy-start | bytes 772
  20.9 42.2 %copy-start.3 = (f32[4,32]{1,0:T(4,128)S(1)}, f32[4,32]{1,0:T(4,128)}, u32[]{:S(2)}) copy-start(f32[4,32]{1,0:T(4,128)} %param.21) | copy-start | bytes 1540
  20.9 63.7 %copy-start.4 = (f32[32]{0:T(128)S(1)}, f32[32]{0:T(128)}, u32[]{:S(2)}) copy-start(f32[32]{0:T(128)} %param.20) | copy-start | bytes 388
  63.0 121.9 %all-reduce.2.cloned.1.call-start = ((), (), s32[]{:S(2)}) async-start(), calls=%async_computation.2 | async-start | bytes 524288 | tf_op jit(solution)/shard_map/psum | solution.py:140
  150.0 0.7 copy-start.1
Sparse Core Ops, SparseCore 0:
  63.1 21.3 reduce-scatter.1
  150.9 33.9 all-reduce.1
where the time goes:
time: 202 us; the launch traced here: 200 us
  matrix products  54.4 us (27%)
  waiting for transfers between devices  47.1 us (23%)
  local copies, waits for them, and re-layouts  38.5 us (19%)
  blocking collectives  36.4 us (18%)
  between operations  14.2 us (7%)
  other arithmetic  8.08 us (4%)
    dot_general x16, matrix products, value_group(): jnp.dot(state_bf, sensitivity_portion, preferred_element_type=jnp.float32)  28 us
    psum x1, waiting for transfers between devices, shards(): summed = lax.psum(direct, 'trade')  25.7 us
    dot_general x16, matrix products, pull_group(): lax.dot_general(value_adjoint, sensitivity_portion, (((1,), (1,)), ((), (...  25.1 us
    reduce_scatter x1, waiting for transfers between devices, shards(): lax.psum_scatter(partial_value, 'trade', scatter_dimension=0, tiled=True)  21.4 us
    all_gather x4, blocking collectives, entering(): everything = jax.tree.map(lambda part: lax.all_gather(part, axis), value)  19.2 us
    all_gather x1, blocking collectives, shards(): gathered = lax.all_gather(net_adjoint, 'trade', axis=0, tiled=True)  13.8 us
    dynamic_slice x16, local copies, waits for them, and re-layouts, value_group(): lax.dynamic_slice_in_dim(signed_notional, opening_offset, cluster_extent, 0)  12.2 us
    dynamic_slice x16, local copies, waits for them, and re-layouts, pull_group(): lax.dynamic_slice_in_dim(signed_notional, opening_offset, cluster_extent, 0)  12.2 us
  transfers between devices with their start and end apart: 2, of which 2 were waited for; matrix products, arithmetic and copies ran while one was open for 0% of the time, Pallas kernels for 0%

commit v1 on v0

--- a/solution.py
+++ b/solution.py
@@ -137,7 +137,9 @@
         0, cluster_ordinal, pull_group, jnp.zeros((row_count, factor_count), jnp.float32)
     )
     direct = direct.reshape(date_count, path_count, factor_count)
-    summed = lax.psum(direct, "trade")
+    summed = direct
+    for hop_ in (1, 2):
+        summed = summed + lax.ppermute(summed, "trade", [(dev, dev ^ hop_) for dev in range(4)])
     shock_gradient = reverse_chain(summed, persistence_ratio)
     return (exposure_profile, shock_gradient)
 

time: 202 us -> 183 us (0.906)
  waiting for transfers between devices: 47.1 us -> 30.2 us
  other arithmetic: 8.08 us -> 5.43 us
    psum x1 -> x0, waiting for transfers between devices: 25.7 us -> none  [shards(): summed = lax.psum(direct, 'trade')]
    ppermute x0 -> x2, waiting for transfers between devices: none -> 8.73 us  [shards(): lax.ppermute(summed, 'trade', [(dev, dev ^ hop_) for dev in range(4)])]
  transfers between devices with their start and end apart: 2 -> 3, of which waited for: 2 -> 3; matrix products, arithmetic and copies ran while one was open for 0% -> 0% of each run, Pallas kernels for 0% -> 0%
where the time goes in v1:
time: 183 us; the launch traced here: 181 us
  matrix products  54.4 us (30%)
  local copies, waits for them, and re-layouts  37.8 us (21%)
  blocking collectives  36.4 us (20%)
  waiting for transfers between devices  30.2 us (17%)
  between operations  14.2 us (8%)
  other arithmetic  5.43 us (3%)
    dot_general x16, matrix products, value_group(): jnp.dot(state_bf, sensitivity_portion, preferred_element_type=jnp.float32)  28 us
    dot_general x16, matrix products, pull_group(): lax.dot_general(value_adjoint, sensitivity_portion, (((1,), (1,)), ((), (...  25 us
    reduce_scatter x1, waiting for transfers between devices, shards(): lax.psum_scatter(partial_value, 'trade', scatter_dimension=0, tiled=True)  21.4 us
    all_gather x4, blocking collectives, entering(): everything = jax.tree.map(lambda part: lax.all_gather(part, axis), value)  19.2 us
    all_gather x1, blocking collectives, shards(): gathered = lax.all_gather(net_adjoint, 'trade', axis=0, tiled=True)  13.8 us
    dynamic_slice x16, local copies, waits for them, and re-layouts, value_group(): lax.dynamic_slice_in_dim(signed_notional, opening_offset, cluster_extent, 0)  12.2 us
    dynamic_slice x16, local copies, waits for them, and re-layouts, pull_group(): lax.dynamic_slice_in_dim(signed_notional, opening_offset, cluster_extent, 0)  12.2 us
    mul x16, local copies, waits for them, and re-layouts, pull_group(): upstream.T[:, :, None]  9.68 us
  transfers between devices with their start and end apart: 3, of which 3 were waited for; matrix products, arithmetic and copies ran while one was open for 0% of the time, Pallas kernels for 0%

profile of v1, /device:TPU:0, one launch (start us, length us, event | category | flops | bytes accessed | tf_op | source)
XLA Modules:
  0.0 181.1 jit_solution(18165399675756211012)
XLA Ops:
  7.2 0.8 multiply_bitcast_fusion
  8.8 5.1 %all-gather = f32[2,1,128]{2,1,0:T(1,128)S(1)} all-gather(f32[1,1,128]{2,1,0:T(1,128)S(1)} %get-tuple-element.550), channel_id=1, replica_groups=mesh['grp'=2,'trade'=4,'date'=2,'path'=2] {'date'}, dimensions={0}, use_global_device_ids=true | all-gather | bytes 1536 | tf_op jit(solution)/shard_map/all_gather | solution.py:13
  13.8 1.0 multiply_add_fusion
  14.8 4.9 %all_gather.20 = f32[2,128,128]{2,1,0:T(8,128)S(1)} all-gather(f32[1,128,128]{2,1,0:T(8,128)S(1)} %multiply_add_fusion), channel_id=1, replica_groups=mesh['grp'=2,'trade'=4,'date'=2,'path'=2] {'date'}, dimensions={0}, use_global_device_ids=true | all-gather | bytes 196608 | tf_op jit(solution)/shard_map/all_gather | solution.py:13
  19.9 0.9 convert_bitcast_fusion.1
  20.9 41.0 %while.57 = (s32[]{:T(128)}, f32[64,512]{1,0:T(8,128)S(1)}, bf16[128,8192]{1,0:T(8,128)(2,1)}, bf16[512,128]{1,0:T(8,128)(2,1)S(1)}, f32[8192]{0:T(1024)}, /*ind...) while((s32[]{:T(128)}, f32[64,512]{1,0:T(8,128)S(1)}, ...), condition=%wide.region_4.5_spmd, body=%wide.region_2.4_spmd.sunk | while | flops 69203976 | bytes 293085 | solution.py:91
  20.9 0.8 dynamic_slice.97
  21.7 1.8 bitcast_reduce_fusion.2
  23.5 0.8 dynamic_slice.97
  24.2 1.8 bitcast_reduce_fusion.2
  26.0 0.8 dynamic_slice.97
  26.8 1.8 bitcast_reduce_fusion.2
  28.6 0.8 dynamic_slice.97
  29.4 1.8 bitcast_reduce_fusion.2
  31.1 0.8 dynamic_slice.97
  31.9 1.8 bitcast_reduce_fusion.2
  33.7 0.8 dynamic_slice.97
  34.5 1.8 bitcast_reduce_fusion.2
  36.3 0.8 dynamic_slice.97
  37.0 1.8 bitcast_reduce_fusion.2
  38.8 0.8 dynamic_slice.97
  39.6 1.7 bitcast_reduce_fusion.2
  41.4 0.8 dynamic_slice.97
  42.2 1.8 bitcast_reduce_fusion.2
  43.9 0.8 dynamic_slice.97
  44.7 1.8 bitcast_reduce_fusion.2
  46.5 0.8 dynamic_slice.97
  47.3 1.8 bitcast_reduce_fusion.2
  49.1 0.8 dynamic_slice.97
  49.8 1.7 bitcast_reduce_fusion.2
  51.6 0.8 dynamic_slice.97
  52.4 1.8 bitcast_reduce_fusion.2
  54.2 0.8 dynamic_slice.97
  55.0 1.8 bitcast_reduce_fusion.2
  56.8 0.8 dynamic_slice.97
  57.5 1.8 bitcast_reduce_fusion.2
  60.1 1.8 bitcast_reduce_fusion.2
  61.9 1.1 fusion.27
  63.1 21.4 %reduce-scatter.2.cloned.1.call-done = f32[32,512]{1,0:T(8,128)} async-done(((f32[128,512]{1,0:T(8,128)}), f32[32,512]{1,0:T(8,128)}) %reduce-scatter.2.cloned.1.call-update) | async-done | bytes 65552 | tf_op jit(solution)/shard_map/reduce_scatter | solution.py:102
  84.6 1.0 bitcast_multiply_fusion
  85.6 13.8 %all_gather.21 = f32[128,512]{1,0:T(8,128)S(1)} all-gather(f32[32,512]{1,0:T(8,128)S(1)} %get-tuple-element.544), channel_id=1, replica_groups=mesh['grp'=2,'trade'=4,'date'=2,'path'=2] {'trade'}, dimensions={0}, use_global_device_ids=true | all-gather | bytes 327680 | tf_op jit(solution)/shard_map/all_gather | solution.py:111
  99.7 50.3 %while.59 = (s32[]{:T(128)}, f32[512,128]{1,0:T(8,128)S(1)}, f32[64,512]{1,0:T(8,128)S(1)}, bf16[128,8192]{1,0:T(8,128)(2,1)}, bf16[512,128]{1,0:T(8,128)(2,1)S(...) while((s32[]{:T(128)}, f32[512,128]{1,0:T(8,128)S(1)}, ...), condition=%wide.region_9.10_spmd.clone, body=%wide.region_8.9_spmd.clone.sunk | while | flops 135921680 | bytes 3063530 | solution.py:136
  101.3 1.6 fusion.50
  104.4 1.6 fusion.50
  107.6 1.6 fusion.50
  110.7 1.6 fusion.50
  113.8 1.6 fusion.50
  117.0 1.6 fusion.50
  120.1 1.6 fusion.50
  123.3 1.6 fusion.50
  126.4 1.6 fusion.50
  129.5 1.6 fusion.50
  132.7 1.6 fusion.50
  135.8 1.6 fusion.50
  139.0 1.6 fusion.50
  142.1 1.6 fusion.50
  145.3 1.6 fusion.50
  147.6 0.8 dynamic_slice.103
  148.4 1.6 fusion.50
  150.1 8.3 %collective-permute-done = f32[4,128,128]{2,1,0:T(8,128)S(1)} collective-permute-done((f32[4,128,128]{2,1,0:T(8,128)S(1)}, f32[4,128,128]{2,1,0:T(8,128)S(1)}, u32[]{:S(2)}, u32[]{:S(2)}) %collective-permute-start) | collective-permute-done | bytes 262176 | tf_op jit(solution)/shard_map/ppermute | solution.py:142
  158.4 1.1 collective-permute-start.1
  159.6 4.2 %all-gather.1 = f32[2,1,128]{2,1,0:T(1,128)S(1)} all-gather(f32[1,1,128]{2,1,0:T(1,128)S(1)} %get-tuple-element.546), channel_id=1, replica_groups=mesh['grp'=2,'trade'=4,'date'=2,'path'=2] {'date'}, dimensions={0}, use_global_device_ids=true | all-gather | bytes 1536 | tf_op jit(solution)/shard_map/all_gather | solution.py:13
  163.9 3.4 %psum.7 = f32[4,32]{0,1:T(8,128)S(1)} all-reduce(f32[4,32]{0,1:T(8,128)S(1)} %bitcast.154), channel_id=1, replica_groups=mesh['grp'=2,'trade'=4,'date'=2,'path'=2] {'path'}, use_global_device_ids=true, to_apply=%region_7.8 | all-reduce | flops 128 | bytes 1024 | tf_op jit(solution)/shard_map/psum | solution.py:105
  168.4 4.9 %all_gather.23 = f32[2,128,128]{2,1,0:T(8,128)S(1)} all-gather(f32[1,128,128]{2,1,0:T(8,128)S(1)} %add_multiply_fusion), channel_id=1, replica_groups=mesh['grp'=2,'trade'=4,'date'=2,'path'=2] {'date'}, dimensions={0}, use_global_device_ids=true | all-gather | bytes 196608 | tf_op jit(solution)/shard_map/all_gather | solution.py:13
  (122 shorter events, 28.3 us)
Async XLA Ops:
  7.2 13.6 %copy-start = (f32[4,128,128]{2,1,0:T(8,128)S(1)}, f32[4,128,128]{2,1,0:T(8,128)}, u32[]{:S(2)}) copy-start(f32[4,128,128]{2,1,0:T(8,128)} %param.15) | copy-start | bytes 786436
  7.2 77.3 %reduce-scatter.2.cloned.1.call-start = ((), (), s32[]{:S(2)}) async-start(), calls=%async_computation.1 | async-start | bytes 327680 | tf_op jit(solution)/shard_map/reduce_scatter | solution.py:102
  20.8 41.0 %copy-start.1 = (s32[64]{0:T(128)S(1)}, s32[64]{0:T(128)}, u32[]{:S(2)}) copy-start(s32[64]{0:T(128)} %param.19) | copy-start | bytes 772
  20.9 42.1 %copy-start.2 = (f32[4,32]{1,0:T(4,128)S(1)}, f32[4,32]{1,0:T(4,128)}, u32[]{:S(2)}) copy-start(f32[4,32]{1,0:T(4,128)} %param.21) | copy-start | bytes 1540
  20.9 63.7 %copy-start.3 = (f32[32]{0:T(128)S(1)}, f32[32]{0:T(128)}, u32[]{:S(2)}) copy-start(f32[32]{0:T(128)} %param.20) | copy-start | bytes 388
  150.0 8.4 %collective-permute-start = (f32[4,128,128]{2,1,0:T(8,128)S(1)}, f32[4,128,128]{2,1,0:T(8,128)S(1)}, u32[]{:S(2)}, u32[]{:S(2)}) collective-permute-start(f32[4,128,128]{2,1,0:T(8,128)S(1)} %bitcast.150), channel_id=1, source_target_pairs={{0,4},{4,0},{8,12},{12,8},{1,5},{5,1},{9,13},{13,9},{2,6},{6,2},{1... | collective-permute-start | bytes 786440 | tf_op jit(solution)/shard_map/ppermute | solution.py:142
  158.4 9.9 %collective-permute-start.1 = (f32[4,128,128]{2,1,0:T(8,128)S(1)}, f32[4,128,128]{2,1,0:T(8,128)S(1)}, u32[]{:S(2)}, u32[]{:S(2)}) collective-permute-start(f32[4,128,128]{2,1,0:T(8,128)S(1)} %add.234), channel_id=1, source_target_pairs={{0,8},{4,12},{8,0},{12,4},{1,9},{5,13},{9,1},{13,5},{2,10},{6,14},... | collective-permute-start | bytes 786440 | tf_op jit(solution)/shard_map/ppermute | solution.py:142
Sparse Core Ops, SparseCore 0:
  63.1 21.3 reduce-scatter.1
